TPU v7x, 128 devices: a whole 4x4x4 slice. The times are simulated.
128 devices in a mesh: blk: 16 (over x_hi, z, core), uly: 8 (over x_lo, y).
Axes of the slice: x: 4 (x_hi: 2, x_lo: 2; x = x_hi * 2 + x_lo), y: 4, z: 4, core: 2. Of those that a mesh axis runs over, the one named last changes fastest.
Arguments:
- queries: bfloat16 [32768, 4096], P(('blk', 'uly')), may hold values from -140 to 140
- keys: bfloat16 [32768, 1024], P(('blk', 'uly')), may hold values from -6 to 6
- values: bfloat16 [32768, 1024], P(('blk', 'uly')), may hold values from -6 to 6
- doc_lengths: int32 [4], replicated, may hold values from 1 to 24576, 32768 in all
- selected: int32 [32, 8], replicated, may hold values from 0 to 30, as said below
Outputs:
- attended: bfloat16 [32768, 4096], P(('blk', 'uly'))
Inputs may be any that keep to these rules, and one draw needn't show every extreme that they name: selected[b, g] <= b, and equals b only for b = 0. For every device index along blk (blocks b with equal b // 2) and every key head, the blocks it selects that lie outside its own 2 blocks lie in distinct blocks of blk, so one other index of blk supplies at most one selected block a key head to it.
All inputs are finite; a program needn't handle non-finite values.
Results may differ from a plain program's by a relative error of at most 0.004.
Values may be sent and summed in bfloat16 or wider, within the bound.
A program may use at most 128 MiB of HBM per device.

v0:
```python
import jax
import jax.numpy as jnp
from jax import lax
from jax.sharding import PartitionSpec as P

HQ = 32
KVH = 8
HD = 128
MB = 1024


def shortened(shard):

    def short(part):
        return part.astype(jnp.bfloat16) if part.dtype == jnp.float32 else part

    return jax.tree.map(short, shard)


def on_device(queries, keys, values, doc_lengths, selected):
    q_heads, k_heads, v_heads = (
        lax.all_to_all(queries, "uly", split_axis=1, concat_axis=0, tiled=True),
        lax.all_to_all(keys, "uly", split_axis=1, concat_axis=0, tiled=True),
        lax.all_to_all(values, "uly", split_axis=1, concat_axis=0, tiled=True),
    )
    shard = k_heads.shape[0]
    kv_dev = k_heads.shape[1] // HD
    per_dev = shard // MB
    group = HQ // KVH
    scale = 1.0 / HD**0.5
    blk_index = lax.axis_index("blk")
    uly_index = lax.axis_index("uly")
    ends = jnp.cumsum(doc_lengths)

    def doc_of(places):
        return jnp.sum((ends <= places[..., None]).astype(jnp.int32), axis=-1)

    column = lax.dynamic_slice_in_dim(selected, uly_index * kv_dev, kv_dev, 1)
    mine = lax.dynamic_slice_in_dim(column, blk_index * per_dev, per_dev, 0)
    offsets = jnp.arange(MB, dtype=jnp.int32)
    k_blocks = k_heads.reshape(per_dev, MB, kv_dev, HD)
    v_blocks = v_heads.reshape(per_dev, MB, kv_dev, HD)
    empty = jnp.zeros((per_dev, kv_dev, MB, HD), jnp.bfloat16)
    k_piece = lax.all_gather(k_heads, "blk", axis=0, tiled=True)
    v_piece = lax.all_gather(v_heads, "blk", axis=0, tiled=True)
    count = k_piece.shape[0]
    wanted_rows = mine[:, :, None] * MB + offsets
    inside = (wanted_rows >= 0) & (wanted_rows < count)
    index = jnp.clip(wanted_rows, 0, count - 1)
    head_rows = jnp.arange(kv_dev, dtype=jnp.int32)[None, :, None]
    k_got = k_piece.reshape(count, kv_dev, HD)[index, head_rows]
    v_got = v_piece.reshape(count, kv_dev, HD)[index, head_rows]
    chosen_k = jnp.where(inside[..., None], k_got, empty)
    chosen_v = jnp.where(inside[..., None], v_got, empty)
    doc_query = doc_of(blk_index * shard + jnp.arange(shard, dtype=jnp.int32)).reshape(per_dev, MB)
    doc_chosen = doc_of(mine[:, :, None] * MB + offsets)
    live = mine != (blk_index * per_dev + jnp.arange(per_dev, dtype=jnp.int32))[:, None]
    q_five = q_heads.reshape(per_dev, MB, kv_dev, group, HD)
    causal = offsets[:, None] >= offsets[None, :]

    def one_block(row):
        q_now = q_five[row, :, 0]
        own_k = k_blocks[row, :, 0]
        own_v = v_blocks[row, :, 0]
        doc_now = doc_query[row]
        own_scores = (
            jnp.einsum("mgd,nd->gmn", q_now, own_k, preferred_element_type=jnp.float32) * scale
        )
        sel_scores = (
            jnp.einsum("mgd,nd->gmn", q_now, chosen_k[row, 0], preferred_element_type=jnp.float32)
            * scale
        )
        own_mask = causal & (doc_now[:, None] == doc_now[None, :])
        sel_mask = (doc_now[:, None] == doc_chosen[row, 0][None, :]) & live[row, 0]
        top = jnp.maximum(
            jnp.max(jnp.where(own_mask, own_scores, -jnp.inf), axis=-1),
            jnp.max(jnp.where(sel_mask, sel_scores, -jnp.inf), axis=-1),
        )
        own_weight = jnp.where(own_mask, jnp.exp(own_scores - top[..., None]), 0.0)
        sel_weight = jnp.where(sel_mask, jnp.exp(sel_scores - top[..., None]), 0.0)
        total = jnp.sum(own_weight, axis=-1) + jnp.sum(sel_weight, axis=-1)
        acc = jnp.einsum(
            "gmn,nd->mgd",
            own_weight.astype(jnp.bfloat16),
            own_v,
            preferred_element_type=jnp.float32,
        )
        acc = acc + jnp.einsum(
            "gmn,nd->mgd",
            sel_weight.astype(jnp.bfloat16),
            chosen_v[row, 0],
            preferred_element_type=jnp.float32,
        )
        output = (acc / jnp.transpose(total)[:, :, None]).astype(jnp.bfloat16)
        results = [output.reshape(MB, group * HD)]
        return jnp.concatenate(results, axis=1)

    blocks = lax.map(one_block, jnp.arange(per_dev, dtype=jnp.int32))
    head_major = blocks.reshape(shard, kv_dev * group * HD)
    return lax.all_to_all(
        shortened(head_major), "uly", split_axis=0, concat_axis=1, tiled=True
    ).astype(head_major.dtype)


def solution(mesh):
    placed = (P(("blk", "uly"), None), P(("blk", "uly"), None), P(("blk", "uly"), None), P(), P())
    return jax.shard_map(
        on_device, mesh=mesh, in_specs=placed, out_specs=P(("blk", "uly"), None), check_vma=False
    )
```

profile of v0, /device:TPU:0, one launch (start us, length us, event | category | flops | bytes accessed | tf_op | source)
XLA Modules:
  0.0 339.3 jit_solution(10035589432104716026)
XLA Ops:
  6.5 1.3 copy.43
  7.8 15.3 %all_to_all.73 = bf16[256,8,128]{0,2,1:T(8,128)(2,1)S(1)} all-to-all(bf16[256,8,128]{0,2,1:T(8,128)(2,1)S(1)} %bitcast.166), channel_id=1, replica_groups=mesh['blk'=16,'uly'=8] {'uly'}, dimensions={1} | all-to-all | bytes 1048576 | tf_op jit(solution)/shard_map/all_to_all | solution.py:24
  23.2 1.0 copy.44
  24.3 0.1 copy_bitcast_fusion.4
  24.4 11.7 %all_to_all.74 = bf16[256,8,128]{2,0,1:T(8,128)(2,1)} all-to-all(bf16[256,8,128]{2,0,1:T(8,128)(2,1)S(1)} %copy_bitcast_fusion.4), channel_id=1, replica_groups=mesh['blk'=16,'uly'=8] {'uly'}, dimensions={1} | all-to-all | bytes 1048576 | tf_op jit(solution)/shard_map/all_to_all | solution.py:23
  36.1 3.1 copy.80
  39.3 3.6 %all-to-all-start.2 = ((bf16[256,8,512]{2,0,1:T(8,128)(2,1)}), bf16[256,8,512]{2,0,1:T(8,128)(2,1)S(1)}, u32[]{:S(2)}, u32[]{:S(2)}) async-start(bf16[256,8,512]{2,0,1:T(8,128)(2,1)} %bitcast.154), calls=%async_computation.2 | async-start | bytes 4194304 | tf_op jit(solution)/shard_map/all_to_all | solution.py:22
  42.9 0.8 dynamic_slice.32
  43.7 0.1 copy.66
  43.8 0.1 multiply_reduce_fusion
  44.0 0.8 reduce-window.8
  44.9 0.1 convert_reduce_fusion.1
  45.0 0.1 convert_reduce_fusion
  45.2 27.4 %all-to-all-done.2 = bf16[256,8,512]{2,0,1:T(8,128)(2,1)S(1)} async-done(((bf16[256,8,512]{2,0,1:T(8,128)(2,1)}), bf16[256,8,512]{2,0,1:T(8,128)(2,1)S(1)}, u32[]{:S(2)}, u32[]{:S(2)}) %all-to-all-start.2) | async-done | bytes 2097184 | tf_op jit(solution)/shard_map/all_to_all | solution.py:22
  72.6 2.1 reshape.225
  74.7 27.1 %all-gather.5.cloned.1.call-done = bf16[32768,128]{1,0:T(8,128)(2,1)} async-done(((bf16[2048,128]{1,0:T(8,128)(2,1)}), bf16[32768,128]{1,0:T(8,128)(2,1)}) %all-gather.5.cloned.1.call-update) | async-done | bytes 8388624 | tf_op jit(solution)/shard_map/all_gather | solution.py:45
  101.8 22.6 %gather_fusion.1 = bf16[2048,128]{1,0:T(8,128)(2,1)S(1)} fusion(bf16[32768,1,128]{2,0,1:T(8,128)(2,1)} %bitcast.157, s32[2048]{0:T(1024)S(1)} %bitcast.150), kind=kCustom, calls=%fused_computation.1 | custom fusion | bytes 1064960 | tf_op jit(solution)/shard_map/gather | solution.py:52
  124.4 0.2 copy.50
  124.7 50.9 %all-gather.3.cloned.1.call-done = bf16[32768,128]{1,0:T(8,128)(2,1)} async-done(((bf16[2048,128]{1,0:T(8,128)(2,1)}), bf16[32768,128]{1,0:T(8,128)(2,1)}) %all-gather.3.cloned.1.call-update) | async-done | bytes 8388624 | tf_op jit(solution)/shard_map/all_gather | solution.py:44
  175.6 22.6 %gather_fusion = bf16[2048,128]{1,0:T(8,128)(2,1)S(1)} fusion(bf16[32768,1,128]{2,0,1:T(8,128)(2,1)} %bitcast.158, s32[2048]{0:T(1024)S(1)} %bitcast.151), kind=kCustom, calls=%fused_computation | custom fusion | bytes 1064960 | tf_op jit(solution)/shard_map/gather | solution.py:51
  198.2 0.2 copy.48
  198.4 1.1 broadcast_select_fusion
  199.5 94.8 %while.11 = (s32[]{:T(128)}, bf16[2,1024,512]{2,1,0:T(8,128)(2,1)}, s32[2]{0:T(128)S(1)}, bf16[2,1024,1,128]{3,1,0,2:T(8,128)(2,1)S(1)}, s32[2,1024]{1,0:T(2,128...) while((s32[]{:T(128)}, bf16[2,1024,512]{2,1,0:T(8,128)(2,1)}, ...), condition=%wide.region_8.9_spmd.clone, body=%wide.region_3.8_spmd.clone.sunk | while | flops 4394049536 | bytes 123986648 | solution.py:98
  199.5 0.6 dynamic_slice.83
  202.0 0.6 constant_dynamic-slice_fusion.10
  202.5 2.5 compare_and_fusion.3
  205.0 1.6 constant_dynamic-slice_fusion.11
  206.6 4.0 %fusion.59 = (f32[4,1024]{1,0:T(4,128)S(1)}, f32[1024,1024,4]{1,0,2:T(8,128)S(1)}) fusion(pred[1024,1024]{0,1:T(8,128)(4,1)S(1)} %get-tuple-element.245, bf16[1,1024,1,4,128]{4,3,1,0,2:T(4,128)(2,1)S(1)} %constant_dynamic-slice_fusion.11, bf16[2,1024,1,128]{3,1,2,0:T(8,128)(2,1)} %get-tuple-element.284, s32[]{:T(128)S(6)} %select_n.115), kind=kOutput, calls=%fused_computation.10.clone.1 | convolution fusion | flops 1086320640 | bytes 19152900 | tf_op jit(solution)/shard_map/while/body/eval_jaxpr/mgd,nd->gmn/dot_general | solution.py:67
  210.6 8.5 %fusion.58 = (f32[4,1024]{1,0:T(4,128)S(1)}, f32[1024,1024,4]{1,0,2:T(8,128)}) fusion(pred[1024,1024]{0,1:T(8,128)(4,1)S(1)} %get-tuple-element.243, bf16[1,1024,1,4,128]{4,3,1,0,2:T(4,128)(2,1)S(1)} %constant_dynamic-slice_fusion.11, bf16[2,1,1024,128]{2,3,1,0:T(8,128)(2,1)} %get-tuple-element.288, s32[]{:T(128)S(6)} %select_n.115), kind=kOutput, calls=%fused_computation.5.clone.1 | convolution fusion | flops 1086320640 | bytes 19152900 | tf_op jit(solution)/shard_map/while/body/eval_jaxpr/mgd,nd->gmn/dot_general | solution.py:70
  219.1 9.9 %fusion.61 = (f32[4,1024]{1,0:T(4,128)S(1)}, f32[4,1024]{1,0:T(4,128)S(1)}) fusion(f32[1024,1024,4]{1,0,2:T(8,128)} %get-tuple-element.244, f32[4,1024]{1,0:T(4,128)S(1)} %max.13, pred[1024,1024]{0,1:T(8,128)(4,1)S(1)} %get-tuple-element.243, f32[1024,1024,4]{1,0,2:T(8,128)S(1)} %get-tuple-element.248, pred[1024,1024]{0,1:T(8,128)(4,1)S(1)} %get-tuple-element.245), kind=kLoop, calls=%fused_computation.15.clone.1 | loop fusion | flops 33546240 | bytes 35700736 | tf_op jit(solution)/shard_map/while/body/eval_jaxpr/reduce_sum | solution.py:81
  229.1 11.0 %fusion.60 = f32[128,4,1024]{2,0,1:T(8,128)} fusion(f32[1024,1024,4]{1,0,2:T(8,128)} %get-tuple-element.244, f32[4,1024]{1,0:T(4,128)S(1)} %max.13, pred[1024,1024]{0,1:T(8,128)(4,1)S(1)} %get-tuple-element.243, bf16[2,1,1024,128]{2,3,1,0:T(8,128)(2,1)} %get-tuple-element.289, s32[]{:T(128)S(6)} %select_n.115), kind=kOutput, calls=%fused_computation.17.clone.1 | convolution fusion | flops 1090519040 | bytes 20201476 | tf_op jit(solution)/shard_map/while/body/eval_jaxpr/gmn,nd->mgd/dot_general | solution.py:88
  240.1 5.2 %fusion.62 = bf16[1024,4,128]{0,2,1:T(8,128)(2,1)S(1)} fusion(f32[128,4,1024]{2,0,1:T(8,128)} %fusion.60, f32[1024,1024,4]{1,0,2:T(8,128)S(1)} %get-tuple-element.248, f32[4,1024]{1,0:T(4,128)S(1)} %max.13, pred[1024,1024]{0,1:T(8,128)(4,1)S(1)} %get-tuple-element.245, f32[1024,4]{0,1:T(4,128)S(1)} %add_bitcast_fusion.2, ...), kind=kOutput, calls=%fused_computation.25.clone.1 | convolution fusion | flops 1092091904 | bytes 21266436 | tf_op jit(solution)/shard_map/while/body/eval_jaxpr/gmn,nd->mgd/dot_general | solution.py:82
  245.3 0.5 copy.87
  245.9 1.0 constant_dynamic-update-slice_fusion.2
  246.9 0.6 dynamic_slice.83
  249.4 0.6 constant_dynamic-slice_fusion.10
  249.9 2.5 compare_and_fusion.3
  252.4 1.6 constant_dynamic-slice_fusion.11
  254.0 4.0 %fusion.59 = (f32[4,1024]{1,0:T(4,128)S(1)}, f32[1024,1024,4]{1,0,2:T(8,128)S(1)}) fusion(pred[1024,1024]{0,1:T(8,128)(4,1)S(1)} %get-tuple-element.245, bf16[1,1024,1,4,128]{4,3,1,0,2:T(4,128)(2,1)S(1)} %constant_dynamic-slice_fusion.11, bf16[2,1024,1,128]{3,1,2,0:T(8,128)(2,1)} %get-tuple-element.284, s32[]{:T(128)S(6)} %select_n.115), kind=kOutput, calls=%fused_computation.10.clone.1 | convolution fusion | flops 1086320640 | bytes 19152900 | tf_op jit(solution)/shard_map/while/body/eval_jaxpr/mgd,nd->gmn/dot_general | solution.py:67
  258.0 8.5 %fusion.58 = (f32[4,1024]{1,0:T(4,128)S(1)}, f32[1024,1024,4]{1,0,2:T(8,128)}) fusion(pred[1024,1024]{0,1:T(8,128)(4,1)S(1)} %get-tuple-element.243, bf16[1,1024,1,4,128]{4,3,1,0,2:T(4,128)(2,1)S(1)} %constant_dynamic-slice_fusion.11, bf16[2,1,1024,128]{2,3,1,0:T(8,128)(2,1)} %get-tuple-element.288, s32[]{:T(128)S(6)} %select_n.115), kind=kOutput, calls=%fused_computation.5.clone.1 | convolution fusion | flops 1086320640 | bytes 19152900 | tf_op jit(solution)/shard_map/while/body/eval_jaxpr/mgd,nd->gmn/dot_general | solution.py:70
  266.5 9.9 %fusion.61 = (f32[4,1024]{1,0:T(4,128)S(1)}, f32[4,1024]{1,0:T(4,128)S(1)}) fusion(f32[1024,1024,4]{1,0,2:T(8,128)} %get-tuple-element.244, f32[4,1024]{1,0:T(4,128)S(1)} %max.13, pred[1024,1024]{0,1:T(8,128)(4,1)S(1)} %get-tuple-element.243, f32[1024,1024,4]{1,0,2:T(8,128)S(1)} %get-tuple-element.248, pred[1024,1024]{0,1:T(8,128)(4,1)S(1)} %get-tuple-element.245), kind=kLoop, calls=%fused_computation.15.clone.1 | loop fusion | flops 33546240 | bytes 35700736 | tf_op jit(solution)/shard_map/while/body/eval_jaxpr/reduce_sum | solution.py:81
  276.5 11.0 %fusion.60 = f32[128,4,1024]{2,0,1:T(8,128)} fusion(f32[1024,1024,4]{1,0,2:T(8,128)} %get-tuple-element.244, f32[4,1024]{1,0:T(4,128)S(1)} %max.13, pred[1024,1024]{0,1:T(8,128)(4,1)S(1)} %get-tuple-element.243, bf16[2,1,1024,128]{2,3,1,0:T(8,128)(2,1)} %get-tuple-element.289, s32[]{:T(128)S(6)} %select_n.115), kind=kOutput, calls=%fused_computation.17.clone.1 | convolution fusion | flops 1090519040 | bytes 20201476 | tf_op jit(solution)/shard_map/while/body/eval_jaxpr/gmn,nd->mgd/dot_general | solution.py:88
  287.4 5.2 %fusion.62 = bf16[1024,4,128]{0,2,1:T(8,128)(2,1)S(1)} fusion(f32[128,4,1024]{2,0,1:T(8,128)} %fusion.60, f32[1024,1024,4]{1,0,2:T(8,128)S(1)} %get-tuple-element.248, f32[4,1024]{1,0:T(4,128)S(1)} %max.13, pred[1024,1024]{0,1:T(8,128)(4,1)S(1)} %get-tuple-element.245, f32[1024,4]{0,1:T(4,128)S(1)} %add_bitcast_fusion.2, ...), kind=kOutput, calls=%fused_computation.25.clone.1 | convolution fusion | flops 1092091904 | bytes 21266436 | tf_op jit(solution)/shard_map/while/body/eval_jaxpr/gmn,nd->mgd/dot_general | solution.py:82
  292.7 0.5 copy.87
  293.2 1.0 constant_dynamic-update-slice_fusion.2
  294.3 31.7 %all_to_all.75 = bf16[8,256,512]{2,1,0:T(8,128)(2,1)S(1)} all-to-all(bf16[8,256,512]{2,1,0:T(8,128)(2,1)} %bitcast.160), channel_id=1, replica_groups=mesh['blk'=16,'uly'=8] {'uly'}, dimensions={0} | all-to-all | bytes 4194304 | tf_op jit(solution)/shard_map/all_to_all | solution.py:100
  326.0 2.4 copy.56
  328.4 4.1 %copy.57 = bf16[256,4096]{1,0:T(8,128)(2,1)} copy(bf16[256,4096]{0,1:T(8,128)(2,1)} %bitcast.156) | data formatting | bytes 4194304 | tf_op jit(solution)/shard_map/all_to_all | solution.py:100
  (29 shorter events, 0.4 us)
Async XLA Ops:
  6.5 17.7 %copy-start = (bf16[256,1024]{1,0:T(8,128)(2,1)S(1)}, bf16[256,1024]{1,0:T(8,128)(2,1)}, u32[]{:S(2)}) copy-start(bf16[256,1024]{1,0:T(8,128)(2,1)} %param.8) | copy-start | bytes 1572868
  6.5 95.3 %all-gather.5.cloned.1.call-start = ((), (), s32[]{:S(2)}) async-start(), calls=%async_computation.5 | async-start | bytes 8912896 | tf_op jit(solution)/shard_map/all_gather | solution.py:45
  24.2 175.3 %copy-start.2 = (bf16[8,256,128]{2,1,0:T(8,128)(2,1)S(1)}, bf16[8,256,128]{2,1,0:T(8,128)(2,1)}, u32[]{:S(2)}) copy-start(bf16[8,256,128]{2,1,0:T(8,128)(2,1)} %copy.44) | copy-start | bytes 1572868
  24.2 151.4 %all-gather.3.cloned.1.call-start = ((), (), s32[]{:S(2)}) async-start(), calls=%async_computation.4 | async-start | bytes 8912896 | tf_op jit(solution)/shard_map/all_gather | solution.py:44
  39.3 33.4 %all-to-all-start.2 = ((bf16[256,8,512]{2,0,1:T(8,128)(2,1)}), bf16[256,8,512]{2,0,1:T(8,128)(2,1)S(1)}, u32[]{:S(2)}, u32[]{:S(2)}) async-start(bf16[256,8,512]{2,0,1:T(8,128)(2,1)} %bitcast.154), calls=%async_computation.2 | async-start | bytes 4194304 | tf_op jit(solution)/shard_map/all_to_all | solution.py:22
  294.3 38.1 %copy-start.1 = (bf16[256,1024]{1,0:T(8,128)(2,1)S(1)}, bf16[256,1024]{1,0:T(8,128)(2,1)}, u32[]{:S(2)}) copy-start(bf16[256,1024]{1,0:T(8,128)(2,1)} %param.8) | copy-start | bytes 1572868
Sparse Core Ops, SparseCore 0:
  24.3 77.4 all-gather.4
  104.3 71.2 all-gather.2
where the time goes:
time: 341 us; the launch traced here: 339 us
  waiting for transfers between devices  105 us (31%)
  local copies, waits for them, and re-layouts  69.3 us (20%)
  blocking collectives  58.8 us (17%)
  matrix products  57.4 us (17%)
  other arithmetic  27.3 us (8%)
  between operations  13.5 us (4%)
  loops' own time  3.8 us (1%)
  starting transfers between devices  3.65 us (1%)
    all_gather x1, waiting for transfers between devices, on_device(): k_piece = lax.all_gather(k_heads, 'blk', axis=0, tiled=True)  50.9 us
    all_to_all x1, blocking collectives, on_device(): lax.all_to_all(shortened(head_major), 'uly', split_axis=0, concat_axis=1,...  31.7 us
    all_to_all x1, waiting for transfers between devices, on_device(): lax.all_to_all(queries, 'uly', split_axis=1, concat_axis=0, tiled=True)  27.4 us
    all_gather x1, waiting for transfers between devices, on_device(): v_piece = lax.all_gather(v_heads, 'blk', axis=0, tiled=True)  27.1 us
    gather x2, local copies, waits for them, and re-layouts, on_device(): v_got = v_piece.reshape(count, kv_dev, HD)[index, head_rows]  22.8 us
    gather x2, local copies, waits for them, and re-layouts, on_device(): k_got = k_piece.reshape(count, kv_dev, HD)[index, head_rows]  22.8 us
    dot_general x2, matrix products, one_block(): jnp.einsum('gmn,nd->mgd', sel_weight.astype(jnp.bfloat16), chosen_v[row,...  21.9 us
    reduce_sum x2, other arithmetic, one_block(): total = jnp.sum(own_weight, axis=-1) + jnp.sum(sel_weight, axis=-1)  19.9 us
  transfers between devices with their start and end apart: 3, of which 3 were waited for; matrix products, arithmetic and copies ran while one was open for 9% of the time, Pallas kernels for 0%

commit v1 on v0

--- a/solution.py
+++ b/solution.py
@@ -41,8 +41,11 @@
     k_blocks = k_heads.reshape(per_dev, MB, kv_dev, HD)
     v_blocks = v_heads.reshape(per_dev, MB, kv_dev, HD)
     empty = jnp.zeros((per_dev, kv_dev, MB, HD), jnp.bfloat16)
-    k_piece = lax.all_gather(k_heads, "blk", axis=0, tiled=True)
-    v_piece = lax.all_gather(v_heads, "blk", axis=0, tiled=True)
+    k_piece, v_piece = jnp.split(
+        lax.all_gather(jnp.concatenate([k_heads, v_heads], axis=1), "blk", axis=0, tiled=True),
+        [k_heads.shape[1]],
+        axis=1,
+    )
     count = k_piece.shape[0]
     wanted_rows = mine[:, :, None] * MB + offsets
     inside = (wanted_rows >= 0) & (wanted_rows < count)

time: 341 us -> 359 us (1.053)
  blocking collectives: 58.8 us -> 31.6 us
  waiting for transfers between devices: 105 us -> 130 us
  local copies, waits for them, and re-layouts: 69.3 us -> 80.7 us
  starting transfers between devices: 3.65 us -> 12.6 us
    all_to_all x2 -> x0, blocking collectives: 27.1 us -> none  [the longest x1 15.3 us: on_device(): lax.all_to_all(values, 'uly', split_axis=1, concat_axis=0, tiled=True)]
    all_to_all x0 -> x2, waiting for transfers between devices: none -> 17.1 us  [the longest x1 8.69 us: on_device(): lax.all_to_all(values, 'uly', split_axis=1, concat_axis=0, tiled=True)]
    reshape x0 -> x1, local copies, waits for them, and re-layouts: none -> 11.3 us  [on_device(): v_got = v_piece.reshape(count, kv_dev, HD)[index, head_rows]]
    all_to_all x0 -> x2, starting transfers between devices: none -> 8.97 us  [the longest x1 5.48 us: on_device(): lax.all_to_all(values, 'uly', split_axis=1, concat_axis=0, tiled=True)]
    all_to_all x1, waiting for transfers between devices: 27.4 us -> 34.2 us  [on_device(): lax.all_to_all(queries, 'uly', split_axis=1, concat_axis=0, tiled=True)]
    all_gather x2 -> x1, waiting for transfers between devices: 78 us -> 78.2 us  [on_device(): lax.all_gather(jnp.concatenate([k_heads, v_heads], axis=1), 'blk', axis=0...]
  transfers between devices with their start and end apart: 3 -> 4, of which waited for: 3 -> 4; matrix products, arithmetic and copies ran while one was open for 9% -> 2% of each run, Pallas kernels for 0% -> 0%
where the time goes in v1:
time: 359 us; the launch traced here: 357 us
  waiting for transfers between devices  130 us (36%)
  local copies, waits for them, and re-layouts  80.7 us (22%)
  matrix products  55.7 us (16%)
  blocking collectives  31.6 us (9%)
  other arithmetic  29.1 us (8%)
  between operations  13.5 us (4%)
  starting transfers between devices  12.6 us (4%)
  loops' own time  4.29 us (1%)
    all_gather x1, waiting for transfers between devices, on_device(): lax.all_gather(jnp.concatenate([k_heads, v_heads], axis=1), 'blk', axis=0...  78.2 us
    all_to_all x1, waiting for transfers between devices, on_device(): lax.all_to_all(queries, 'uly', split_axis=1, concat_axis=0, tiled=True)  34.2 us
    all_to_all x1, blocking collectives, on_device(): lax.all_to_all(shortened(head_major), 'uly', split_axis=0, concat_axis=1,...  31.6 us
    gather x2, local copies, waits for them, and re-layouts, on_device(): k_got = k_piece.reshape(count, kv_dev, HD)[index, head_rows]  22.8 us
    gather x2, local copies, waits for them, and re-layouts, on_device(): v_got = v_piece.reshape(count, kv_dev, HD)[index, head_rows]  22.7 us
    dot_general x2, matrix products, one_block(): jnp.einsum('gmn,nd->mgd', sel_weight.astype(jnp.bfloat16), chosen_v[row,...  22 us
    reduce_sum x2, other arithmetic, one_block(): total = jnp.sum(own_weight, axis=-1) + jnp.sum(sel_weight, axis=-1)  19.9 us
    dot_general x2, matrix products, one_block(): jnp.einsum('mgd,nd->gmn', q_now, chosen_k[row, 0], preferred_element_type...  17 us
  transfers between devices with their start and end apart: 4, of which 4 were waited for; matrix products, arithmetic and copies ran while one was open for 2% of the time, Pallas kernels for 0%

profile of v1, /device:TPU:0, one launch (start us, length us, event | category | flops | bytes accessed | tf_op | source)
XLA Modules:
  0.0 357.2 jit_solution(13733822805454754690)
XLA Ops:
  6.5 2.2 copy.43
  8.7 5.5 %all-to-all-start = ((bf16[256,8,128]{0,2,1:T(8,128)(2,1)}), bf16[256,8,128]{0,2,1:T(8,128)(2,1)S(1)}, u32[]{:S(2)}, u32[]{:S(2)}) async-start(bf16[256,8,128]{0,2,1:T(8,128)(2,1)} %bitcast.162), calls=%async_computation | async-start | bytes 1048576 | tf_op jit(solution)/shard_map/all_to_all | solution.py:24
  14.2 0.9 copy_bitcast_fusion.4
  15.1 8.7 %all-to-all-done = bf16[256,8,128]{0,2,1:T(8,128)(2,1)S(1)} async-done(((bf16[256,8,128]{0,2,1:T(8,128)(2,1)}), bf16[256,8,128]{0,2,1:T(8,128)(2,1)S(1)}, u32[]{:S(2)}, u32[]{:S(2)}) %all-to-all-start) | async-done | bytes 524320 | tf_op jit(solution)/shard_map/all_to_all | solution.py:24
  23.8 3.5 all-to-all-start.1
  27.3 1.0 copy.44
  28.4 8.4 %all-to-all-done.1 = bf16[256,8,128]{2,0,1:T(8,128)(2,1)S(1)} async-done(((bf16[256,8,128]{2,0,1:T(8,128)(2,1)}), bf16[256,8,128]{2,0,1:T(8,128)(2,1)S(1)}, u32[]{:S(2)}, u32[]{:S(2)}) %all-to-all-start.1) | async-done | bytes 524320 | tf_op jit(solution)/shard_map/all_to_all | solution.py:23
  36.8 2.3 pad_maximum_fusion
  39.2 1.6 copy.80
  40.7 3.6 %all-to-all-start.2 = ((bf16[256,8,512]{2,0,1:T(8,128)(2,1)}), bf16[256,8,512]{2,0,1:T(8,128)(2,1)S(1)}, u32[]{:S(2)}, u32[]{:S(2)}) async-start(bf16[256,8,512]{2,0,1:T(8,128)(2,1)} %bitcast.156), calls=%async_computation.2 | async-start | bytes 4194304 | tf_op jit(solution)/shard_map/all_to_all | solution.py:22
  44.3 0.8 dynamic_slice.32
  45.2 0.1 multiply_reduce_fusion
  45.5 0.2 reduce-window.8
  46.0 34.2 %all-to-all-done.2 = bf16[256,8,512]{2,0,1:T(8,128)(2,1)S(1)} async-done(((bf16[256,8,512]{2,0,1:T(8,128)(2,1)}), bf16[256,8,512]{2,0,1:T(8,128)(2,1)S(1)}, u32[]{:S(2)}, u32[]{:S(2)}) %all-to-all-start.2) | async-done | bytes 2097184 | tf_op jit(solution)/shard_map/all_to_all | solution.py:22
  80.2 2.0 reshape.225
  82.3 78.2 %all-gather.2.cloned.1.call-done = bf16[32768,256]{1,0:T(8,128)(2,1)} async-done(((bf16[2048,256]{1,0:T(8,128)(2,1)}), bf16[32768,256]{1,0:T(8,128)(2,1)}) %all-gather.2.cloned.1.call-update) | async-done | bytes 16777232 | tf_op jit(solution)/shard_map/all_gather | solution.py:45
  160.5 11.3 %slice_bitcast_fusion = (bf16[32768,1,128]{2,0,1:T(8,128)(2,1)}, bf16[32768,1,128]{2,0,1:T(8,128)(2,1)}) fusion(bf16[32768,256]{1,0:T(8,128)(2,1)} %all-gather.2.cloned.1.call-done), kind=kLoop, calls=%fused_computation.51 | loop fusion | bytes 33554432 | tf_op jit(solution)/shard_map/reshape | solution.py:55
  171.8 22.5 %gather_fusion = bf16[2048,128]{1,0:T(8,128)(2,1)S(1)} fusion(bf16[32768,1,128]{2,0,1:T(8,128)(2,1)} %get-tuple-element.167, s32[2048]{0:T(1024)S(1)} %bitcast.152), kind=kCustom, calls=%fused_computation | custom fusion | bytes 1064960 | tf_op jit(solution)/shard_map/gather | solution.py:54
  194.3 0.2 copy.49
  194.6 22.5 %gather_fusion.1 = bf16[2048,128]{1,0:T(8,128)(2,1)S(1)} fusion(bf16[32768,1,128]{2,0,1:T(8,128)(2,1)} %get-tuple-element.166, s32[2048]{0:T(1024)S(1)} %bitcast.153), kind=kCustom, calls=%fused_computation.1 | custom fusion | bytes 1064960 | tf_op jit(solution)/shard_map/gather | solution.py:55
  217.1 0.2 copy.50
  217.3 1.1 broadcast_select_fusion
  218.4 93.9 %while.11 = (s32[]{:T(128)}, bf16[2,1024,512]{2,1,0:T(8,128)(2,1)}, s32[2]{0:T(128)S(1)}, bf16[2,1024,1,128]{3,1,0,2:T(8,128)(2,1)}, s32[2,1024]{1,0:T(2,128)S(1...) while((s32[]{:T(128)}, bf16[2,1024,512]{2,1,0:T(8,128)(2,1)}, ...), condition=%wide.region_8.9_spmd.clone, body=%wide.region_3.8_spmd.clone.sunk | while | flops 4394049536 | bytes 123986648 | solution.py:101
  218.4 0.7 dynamic_slice.83
  221.1 0.6 constant_dynamic-slice_fusion.10
  221.7 2.5 compare_and_fusion.3
  224.3 1.6 constant_dynamic-slice_fusion.11
  225.9 3.1 fusion.59
  228.9 8.5 %fusion.58 = (f32[4,1024]{1,0:T(4,128)S(1)}, f32[1024,1024,4]{1,0,2:T(8,128)}) fusion(pred[1024,1024]{0,1:T(8,128)(4,1)S(1)} %get-tuple-element.245, bf16[1,1024,1,4,128]{4,3,1,0,2:T(4,128)(2,1)S(1)} %constant_dynamic-slice_fusion.11, bf16[2,1,1024,128]{2,3,1,0:T(8,128)(2,1)} %get-tuple-element.290, s32[]{:T(128)S(6)} %select_n.115), kind=kOutput, calls=%fused_computation.5.clone.1 | convolution fusion | flops 1086320640 | bytes 19152900 | tf_op jit(solution)/shard_map/while/body/eval_jaxpr/mgd,nd->gmn/dot_general | solution.py:73
  237.5 9.9 %fusion.61 = (f32[4,1024]{1,0:T(4,128)S(1)}, f32[4,1024]{1,0:T(4,128)S(1)}) fusion(f32[1024,1024,4]{1,0,2:T(8,128)} %get-tuple-element.246, f32[4,1024]{1,0:T(4,128)S(1)} %max.13, pred[1024,1024]{0,1:T(8,128)(4,1)S(1)} %get-tuple-element.245, f32[1024,1024,4]{1,0,2:T(8,128)S(1)} %get-tuple-element.250, pred[1024,1024]{0,1:T(8,128)(4,1)S(1)} %get-tuple-element.247), kind=kLoop, calls=%fused_computation.15.clone.1 | loop fusion | flops 33546240 | bytes 35700736 | tf_op jit(solution)/shard_map/while/body/eval_jaxpr/reduce_sum | solution.py:84
  247.4 11.0 %fusion.60 = f32[128,4,1024]{2,0,1:T(8,128)} fusion(f32[1024,1024,4]{1,0,2:T(8,128)} %get-tuple-element.246, f32[4,1024]{1,0:T(4,128)S(1)} %max.13, pred[1024,1024]{0,1:T(8,128)(4,1)S(1)} %get-tuple-element.245, bf16[2,1,1024,128]{2,3,1,0:T(8,128)(2,1)} %get-tuple-element.291, s32[]{:T(128)S(6)} %select_n.115), kind=kOutput, calls=%fused_computation.17.clone.1 | convolution fusion | flops 1090519040 | bytes 20201476 | tf_op jit(solution)/shard_map/while/body/eval_jaxpr/gmn,nd->mgd/dot_general | solution.py:91
  258.4 5.3 %fusion.62 = bf16[1024,4,128]{0,2,1:T(8,128)(2,1)S(1)} fusion(f32[128,4,1024]{2,0,1:T(8,128)} %fusion.60, f32[1024,1024,4]{1,0,2:T(8,128)S(1)} %get-tuple-element.250, f32[4,1024]{1,0:T(4,128)S(1)} %max.13, pred[1024,1024]{0,1:T(8,128)(4,1)S(1)} %get-tuple-element.247, f32[1024,4]{0,1:T(4,128)S(1)} %add_bitcast_fusion.2, ...), kind=kOutput, calls=%fused_computation.25.clone.1 | convolution fusion | flops 1092091904 | bytes 21266436 | tf_op jit(solution)/shard_map/while/body/eval_jaxpr/gmn,nd->mgd/dot_general | solution.py:85
  263.7 0.5 copy.87
  264.3 1.0 constant_dynamic-update-slice_fusion.2
  265.3 0.7 dynamic_slice.83
  268.1 0.6 constant_dynamic-slice_fusion.10
  268.7 2.5 compare_and_fusion.3
  271.2 1.6 constant_dynamic-slice_fusion.11
  272.8 3.0 fusion.59
  275.9 8.5 %fusion.58 = (f32[4,1024]{1,0:T(4,128)S(1)}, f32[1024,1024,4]{1,0,2:T(8,128)}) fusion(pred[1024,1024]{0,1:T(8,128)(4,1)S(1)} %get-tuple-element.245, bf16[1,1024,1,4,128]{4,3,1,0,2:T(4,128)(2,1)S(1)} %constant_dynamic-slice_fusion.11, bf16[2,1,1024,128]{2,3,1,0:T(8,128)(2,1)} %get-tuple-element.290, s32[]{:T(128)S(6)} %select_n.115), kind=kOutput, calls=%fused_computation.5.clone.1 | convolution fusion | flops 1086320640 | bytes 19152900 | tf_op jit(solution)/shard_map/while/body/eval_jaxpr/mgd,nd->gmn/dot_general | solution.py:73
  284.4 9.9 %fusion.61 = (f32[4,1024]{1,0:T(4,128)S(1)}, f32[4,1024]{1,0:T(4,128)S(1)}) fusion(f32[1024,1024,4]{1,0,2:T(8,128)} %get-tuple-element.246, f32[4,1024]{1,0:T(4,128)S(1)} %max.13, pred[1024,1024]{0,1:T(8,128)(4,1)S(1)} %get-tuple-element.245, f32[1024,1024,4]{1,0,2:T(8,128)S(1)} %get-tuple-element.250, pred[1024,1024]{0,1:T(8,128)(4,1)S(1)} %get-tuple-element.247), kind=kLoop, calls=%fused_computation.15.clone.1 | loop fusion | flops 33546240 | bytes 35700736 | tf_op jit(solution)/shard_map/while/body/eval_jaxpr/reduce_sum | solution.py:84
  294.4 11.0 %fusion.60 = f32[128,4,1024]{2,0,1:T(8,128)} fusion(f32[1024,1024,4]{1,0,2:T(8,128)} %get-tuple-element.246, f32[4,1024]{1,0:T(4,128)S(1)} %max.13, pred[1024,1024]{0,1:T(8,128)(4,1)S(1)} %get-tuple-element.245, bf16[2,1,1024,128]{2,3,1,0:T(8,128)(2,1)} %get-tuple-element.291, s32[]{:T(128)S(6)} %select_n.115), kind=kOutput, calls=%fused_computation.17.clone.1 | convolution fusion | flops 1090519040 | bytes 20201476 | tf_op jit(solution)/shard_map/while/body/eval_jaxpr/gmn,nd->mgd/dot_general | solution.py:91
  305.4 5.3 %fusion.62 = bf16[1024,4,128]{0,2,1:T(8,128)(2,1)S(1)} fusion(f32[128,4,1024]{2,0,1:T(8,128)} %fusion.60, f32[1024,1024,4]{1,0,2:T(8,128)S(1)} %get-tuple-element.250, f32[4,1024]{1,0:T(4,128)S(1)} %max.13, pred[1024,1024]{0,1:T(8,128)(4,1)S(1)} %get-tuple-element.247, f32[1024,4]{0,1:T(4,128)S(1)} %add_bitcast_fusion.2, ...), kind=kOutput, calls=%fused_computation.25.clone.1 | convolution fusion | flops 1092091904 | bytes 21266436 | tf_op jit(solution)/shard_map/while/body/eval_jaxpr/gmn,nd->mgd/dot_general | solution.py:85
  310.7 0.5 copy.87
  311.2 1.0 constant_dynamic-update-slice_fusion.2
  312.3 31.6 %all_to_all.73 = bf16[8,256,512]{2,1,0:T(8,128)(2,1)S(1)} all-to-all(bf16[8,256,512]{2,1,0:T(8,128)(2,1)} %bitcast.160), channel_id=1, replica_groups=mesh['blk'=16,'uly'=8] {'uly'}, dimensions={0} | all-to-all | bytes 4194304 | tf_op jit(solution)/shard_map/all_to_all | solution.py:103
  343.9 2.4 copy.56
  346.3 4.1 %copy.57 = bf16[256,4096]{1,0:T(8,128)(2,1)} copy(bf16[256,4096]{0,1:T(8,128)(2,1)} %bitcast.158) | data formatting | bytes 4194304 | tf_op jit(solution)/shard_map/all_to_all | solution.py:103
  (36 shorter events, 0.7 us)
Async XLA Ops:
  6.5 7.7 %copy-start = (bf16[256,1024]{1,0:T(8,128)(2,1)S(1)}, bf16[256,1024]{1,0:T(8,128)(2,1)}, u32[]{:S(2)}) copy-start(bf16[256,1024]{1,0:T(8,128)(2,1)} %param.8) | copy-start | bytes 1572868
  6.5 32.6 %copy-start.2 = (bf16[256,4096]{1,0:T(8,128)(2,1)S(1)}, bf16[256,4096]{1,0:T(8,128)(2,1)}, u32[]{:S(2)}) copy-start(bf16[256,4096]{1,0:T(8,128)(2,1)} %param.7) | copy-start | bytes 6291460
  6.5 38.9 %copy-start.5 = (s32[4]{0:T(128)S(1)}, s32[4]{0:T(128)}, u32[]{:S(2)}) copy-start(s32[4]{0:T(128)} %param.10) | copy-start | bytes 52
  8.7 15.1 %all-to-all-start = ((bf16[256,8,128]{0,2,1:T(8,128)(2,1)}), bf16[256,8,128]{0,2,1:T(8,128)(2,1)S(1)}, u32[]{:S(2)}, u32[]{:S(2)}) async-start(bf16[256,8,128]{0,2,1:T(8,128)(2,1)} %bitcast.162), calls=%async_computation | async-start | bytes 1048576 | tf_op jit(solution)/shard_map/all_to_all | solution.py:24
  23.8 13.0 %all-to-all-start.1 = ((bf16[256,8,128]{2,0,1:T(8,128)(2,1)}), bf16[256,8,128]{2,0,1:T(8,128)(2,1)S(1)}, u32[]{:S(2)}, u32[]{:S(2)}) async-start(bf16[256,8,128]{2,0,1:T(8,128)(2,1)} %copy_bitcast_fusion.4), calls=%async_computation.1 | async-start | bytes 1048576 | tf_op jit(solution)/shard_map/all_to_all | solution.py:23
  27.3 133.2 %all-gather.2.cloned.1.call-start = ((), (), s32[]{:S(2)}) async-start(), calls=%async_computation.4 | async-start | bytes 17825792 | tf_op jit(solution)/shard_map/all_gather | solution.py:45
  36.8 8.6 %copy-start.3 = (bf16[256,8,128]{2,0,1:T(8,128)(2,1)}, bf16[256,8,128]{2,0,1:T(8,128)(2,1)S(1)}, u32[]{:S(2)}) copy-start(bf16[256,8,128]{2,0,1:T(8,128)(2,1)S(1)} %all-to-all-done.1) | copy-start | bytes 1572868
  40.7 39.5 %all-to-all-start.2 = ((bf16[256,8,512]{2,0,1:T(8,128)(2,1)}), bf16[256,8,512]{2,0,1:T(8,128)(2,1)S(1)}, u32[]{:S(2)}, u32[]{:S(2)}) async-start(bf16[256,8,512]{2,0,1:T(8,128)(2,1)} %bitcast.156), calls=%async_computation.2 | async-start | bytes 4194304 | tf_op jit(solution)/shard_map/all_to_all | solution.py:22
  171.8 46.6 %copy-start.4 = (bf16[256,8,128]{2,0,1:T(8,128)(2,1)S(1)}, bf16[256,8,128]{2,0,1:T(8,128)(2,1)}, u32[]{:S(2)}) copy-start(bf16[256,8,128]{2,0,1:T(8,128)(2,1)} %copy-done.3) | copy-start | bytes 1572868
  312.3 38.1 %copy-start.1 = (bf16[256,1024]{1,0:T(8,128)(2,1)S(1)}, bf16[256,1024]{1,0:T(8,128)(2,1)}, u32[]{:S(2)}) copy-start(bf16[256,1024]{1,0:T(8,128)(2,1)} %param.8) | copy-start | bytes 1572868
Sparse Core Ops, SparseCore 0:
  39.3 121.1 all-gather.1
